TPU v7x, 256 devices: a whole 4x4x8 slice. The times are simulated.
256 devices in a mesh: layer: 4 (over z_hi, core), doc: 64 (over y, x, z_lo).
Axes of the slice: x: 4, y: 4, z: 8 (z_hi: 2, z_lo: 4; z = z_hi * 4 + z_lo), core: 2. Of those that a mesh axis runs over, the one named last changes fastest.
Arguments:
- query_grads: bfloat16 [4, 256, 4096], P('layer', 'doc'), may hold values from -6 to 6
- stored_grads: bfloat16 [4, 65536, 4096], P('layer', 'doc'), may hold values from -0.0234375 to 0.0234375
- basis_in: float32 [4, 64, 64], P('layer'), may hold values from -0.75 to 0.75
- basis_out: float32 [4, 64, 64], P('layer'), may hold values from -0.75 to 0.75
- eigen_values: float32 [4, 64, 64], P('layer'), may hold values from 0.02 to 4
- layer_mask: int32 [256, 4], P(None, 'layer'), may hold values 0 or 1
- doc_counts: int32 [64], P('doc'), may hold values from 1 to 1024, 32768 in all
Outputs:
- scores: float32 [256, 65536], P('layer', 'doc')
Inputs may be any that keep to these rules, and one draw needn't show every extreme that they name: `doc_counts`: the counts sum to 32768 and the largest equals 1024.
All inputs are finite; a program needn't handle non-finite values. No bound on the sum of `layer_mask` or of `doc_counts` on one device may be relied on, other than what follows from the above.
Results may differ from a plain program's by a relative error of at most 0.0029.
Values may be sent and summed in bfloat16 or wider, within the bound.
No kernel may reach another device: no remote copies, remote signals or barrier semaphores. Data moves between devices by JAX's collectives and lax.ppermute only.
A program may use at most 64 MiB of HBM per device.

v0:
```python
import jax
import jax.numpy as jnp
from jax import lax
from jax.sharding import PartitionSpec as P

damping = 0.1


def precondition(gradients, basis_in, basis_out, eigen_values):
    row_count = gradients.shape[0]
    grid_blocks = gradients.astype(jnp.float32).reshape(
        row_count, basis_out.shape[0], basis_in.shape[0]
    )
    rotated = jnp.einsum(
        "xi,qxy,yj->qij", basis_out, grid_blocks, basis_in, precision=lax.Precision.HIGHEST
    )
    scaled = rotated / (eigen_values + damping)
    restored = jnp.einsum(
        "bi,qij,aj->qba", basis_out, scaled, basis_in, precision=lax.Precision.HIGHEST
    )
    return restored.reshape(row_count, -1).astype(jnp.bfloat16)


def on_device(query_grads, stored_grads, basis_in, basis_out, eigen_values, layer_mask, doc_counts):
    stored = stored_grads[0]
    base_in = basis_in[0]
    base_out = basis_out[0]
    eigens = eigen_values[0]
    row_weights = layer_mask[:, 0].astype(jnp.bfloat16)
    own_rows = precondition(query_grads[0], base_in, base_out, eigens)
    masked = lax.all_gather(own_rows, "doc", axis=0, tiled=True) * row_weights[:, None]
    score_tiles = lax.dot_general(
        masked, stored, (((1,), (1,)), ((), ())), preferred_element_type=jnp.float32
    )
    live_slots = jnp.arange(stored.shape[0], dtype=jnp.int32) < doc_counts[0]
    score_tiles = jnp.where(live_slots[None, :], score_tiles, jnp.zeros_like(score_tiles))
    return lax.psum_scatter(score_tiles, "layer", scatter_dimension=0, tiled=True)


def solution(mesh):
    in_specs = (
        P("layer", "doc", None),
        P("layer", "doc", None),
        P("layer", None, None),
        P("layer", None, None),
        P("layer", None, None),
        P(None, "layer"),
        P("doc"),
    )
    out_specs = P("layer", "doc")
    return jax.shard_map(
        on_device, mesh=mesh, in_specs=in_specs, out_specs=out_specs, check_vma=False
    )
```

profile of v0, /device:TPU:1, one launch (start us, length us, event | category | flops | bytes accessed | tf_op | source)
XLA Modules:
  0.0 424.5 jit_solution(11922888940631086043)
XLA Ops:
  6.5 0.0 copy-start
  6.5 0.0 all-gather.3.cloned.1.call-start
  6.5 0.9 reshape.10
  7.4 0.8 add_bitcast_fusion
  8.2 0.0 copy-done
  8.2 0.3 fusion.13
  8.5 1.1 convolution_divide_fusion
  9.6 0.3 fusion.11
  9.9 1.0 convolution_convert_fusion
  10.9 0.7 reshape.11
  11.6 0.0 all-gather.3.cloned.1.call-update
  11.7 0.0 reduce-scatter.2.cloned.1.call-start
  12.4 0.7 convert_reduce_fusion
  13.1 306.5 %all-gather.3.cloned.1.call-done = bf16[64,4,4096]{2,1,0:T(4,128)(2,1)} async-done(((bf16[1,4,4096]{2,1,0:T(4,128)(2,1)}), bf16[64,4,4096]{2,1,0:T(4,128)(2,1)}) %all-gather.3.cloned.1.call-update) | async-done | bytes 2097168 | tf_op jit(solution)/shard_map/all_gather | solution.py:31
  319.6 2.5 reshape.12
  322.1 6.7 %fusion.3 = f32[256,1024]{1,0:T(8,128)} fusion(bf16[1,1024,4096]{2,1,0:T(8,128)(2,1)} %param.8, bf16[256,4096]{1,0:T(8,128)(2,1)S(1)} %reshape.12, bf16[256]{0:T(256)(128)(2,1)S(1)} %convert_reduce_fusion, pred[1024]{0:T(1024)(128)(4,1)S(1)} %iota_compare_fusion), kind=kOutput, calls=%fused_computation.3 | convolution fusion | flops 2148794368 | bytes 11535872 | tf_op jit(solution)/shard_map/dot_general | solution.py:32
  328.9 0.0 reduce-scatter.2.cloned.1.call-update
  328.9 88.8 %reduce-scatter.2.cloned.1.call-done = f32[64,1024]{1,0:T(8,128)} async-done(((f32[256,1024]{1,0:T(8,128)}), f32[64,1024]{1,0:T(8,128)}) %reduce-scatter.2.cloned.1.call-update) | async-done | bytes 262160 | tf_op jit(solution)/shard_map/reduce_scatter | solution.py:37
  (1 shorter events, 0.0 us)
Async XLA Ops:
  6.5 1.7 copy-start
  6.5 313.1 %all-gather.3.cloned.1.call-start = ((), (), s32[]{:S(2)}) async-start(), calls=%async_computation.2 | async-start | bytes 2129920 | tf_op jit(solution)/shard_map/all_gather | solution.py:31
  11.7 406.0 %reduce-scatter.2.cloned.1.call-start = ((), (), s32[]{:S(2)}) async-start(), calls=%async_computation.1 | async-start | bytes 1310720 | tf_op jit(solution)/shard_map/reduce_scatter | solution.py:37
Sparse Core Ops, SparseCore 0:
  11.8 307.7 all-gather.2
  329.0 88.6 reduce-scatter.1
where the time goes:
time: 425 us
  waiting for transfers between devices  395 us (93%)
  between operations  14.1 us (3%)
  matrix products  9.42 us (2%)
    all_gather x1, waiting for transfers between devices, on_device(): lax.all_gather(own_rows, 'doc', axis=0, tiled=True) * row_weights[:, None]  307 us
    reduce_scatter x1, waiting for transfers between devices, on_device(): lax.psum_scatter(score_tiles, 'layer', scatter_dimension=0, tiled=True)  88.8 us
  transfers between devices with their start and end apart: 2, of which 2 were waited for; matrix products, arithmetic and copies ran while one was open for 0% of the time, Pallas kernels for 0%

commit v1 on v0

--- a/solution.py
+++ b/solution.py
@@ -4,6 +4,15 @@
 from jax.sharding import PartitionSpec as P
 
 damping = 0.1
+
+
+def begin_sections(local_values):
+    return jnp.concatenate(
+        lax.all_to_all(
+            jnp.stack([local_values for _ in range(lax.axis_size("doc"))], 0), "doc", 0, 0
+        ),
+        0,
+    )
 
 
 def precondition(gradients, basis_in, basis_out, eigen_values):
@@ -28,7 +37,7 @@
     eigens = eigen_values[0]
     row_weights = layer_mask[:, 0].astype(jnp.bfloat16)
     own_rows = precondition(query_grads[0], base_in, base_out, eigens)
-    masked = lax.all_gather(own_rows, "doc", axis=0, tiled=True) * row_weights[:, None]
+    masked = begin_sections(own_rows) * row_weights[:, None]
     score_tiles = lax.dot_general(
         masked, stored, (((1,), (1,)), ((), ())), preferred_element_type=jnp.float32
     )

time: 425 us -> 138 us (0.32)
  waiting for transfers between devices: 395 us -> 92.4 us
  starting transfers between devices: 0.04 us -> 12.7 us
    all_gather x1 -> x0, waiting for transfers between devices: 307 us -> none  [on_device(): lax.all_gather(own_rows, 'doc', axis=0, tiled=True) * row_weights[:, None]]
    all_to_all x0 -> x1, waiting for transfers between devices: none -> 49.5 us  [begin_sections(): lax.all_to_all(jnp.stack([local_values for _ in range(lax.axis_size('doc'...]
    reduce_scatter x1, waiting for transfers between devices: 88.8 us -> 42.9 us  [on_device(): lax.psum_scatter(score_tiles, 'layer', scatter_dimension=0, tiled=True)]
    all_to_all x0 -> x1, starting transfers between devices: none -> 12.7 us  [begin_sections(): lax.all_to_all(jnp.stack([local_values for _ in range(lax.axis_size('doc'...]
where the time goes in v1:
time: 138 us
  waiting for transfers between devices  92.4 us (67%)
  between operations  14.1 us (10%)
  starting transfers between devices  12.7 us (9%)
  matrix products  9.41 us (7%)
  local copies, waits for them, and re-layouts  6.01 us (4%)
  other arithmetic  3.12 us (2%)
    all_to_all x1, waiting for transfers between devices, begin_sections(): lax.all_to_all(jnp.stack([local_values for _ in range(lax.axis_size('doc'...  49.5 us
    reduce_scatter x1, waiting for transfers between devices, on_device(): lax.psum_scatter(score_tiles, 'layer', scatter_dimension=0, tiled=True)  42.9 us
    all_to_all x1, starting transfers between devices, begin_sections(): lax.all_to_all(jnp.stack([local_values for _ in range(lax.axis_size('doc'...  12.7 us
    dot_general x1, matrix products, on_device(): lax.dot_general(masked, stored, (((1,), (1,)), ((), ())), preferred_eleme...  6.72 us
  transfers between devices with their start and end apart: 2, of which 2 were waited for; matrix products, arithmetic and copies ran while one was open for 0% of the time, Pallas kernels for 0%

profile of v1, /device:TPU:1, one launch (start us, length us, event | category | flops | bytes accessed | tf_op | source)
XLA Modules:
  0.0 137.8 jit_solution(9609637693861954365)
XLA Ops:
  6.5 0.0 copy-start
  6.5 0.9 reshape.20
  7.4 0.8 add_bitcast_fusion
  8.2 0.0 copy-done
  8.2 0.3 fusion.9
  8.5 1.1 convolution_divide_fusion
  9.6 0.3 fusion.7
  9.9 1.0 convolution_convert_fusion
  10.9 0.1 convert_element_type.14
  11.0 2.4 %stack.2 = bf16[64,4,4096]{2,1,0:T(4,128)(2,1)} broadcast(bf16[4,4096]{1,0:T(4,128)(2,1)S(1)} %convert_element_type.14), dimensions={1,2} | broadcast | bytes 2129920 | tf_op jit(solution)/shard_map/stack | solution.py:12
  13.4 0.0 copy-start.1
  13.4 12.7 %all-to-all-start = ((bf16[64,4,4096]{2,1,0:T(4,128)(2,1)}), bf16[64,4,4096]{2,1,0:T(4,128)(2,1)S(1)}, u32[]{:S(2)}, u32[]{:S(2)}) async-start(bf16[64,4,4096]{2,1,0:T(4,128)(2,1)} %stack.2), calls=%async_computation | async-start | bytes 4194304 | tf_op jit(solution)/shard_map/all_to_all | solution.py:11
  26.1 0.0 reduce-scatter.2.cloned.1.call-start
  26.1 0.0 copy-done.1
  26.1 0.1 mul.13
  26.9 49.5 %all-to-all-done = bf16[64,4,4096]{2,1,0:T(4,128)(2,1)S(1)} async-done(((bf16[64,4,4096]{2,1,0:T(4,128)(2,1)}), bf16[64,4,4096]{2,1,0:T(4,128)(2,1)S(1)}, u32[]{:S(2)}, u32[]{:S(2)}) %all-to-all-start) | async-done | bytes 2097184 | tf_op jit(solution)/shard_map/all_to_all | solution.py:11
  76.4 2.3 %broadcast_multiply_fusion = bf16[64,4,4096]{2,1,0:T(4,128)(2,1)} fusion(bf16[64,4,4096]{2,1,0:T(4,128)(2,1)S(1)} %all-to-all-done, bf16[64,4]{1,0:T(8,128)(2,1)S(1)} %mul.13), kind=kLoop, calls=%fused_computation.5 | loop fusion | flops 1048576 | bytes 4194816 | tf_op jit(solution)/shard_map/mul | solution.py:40
  78.8 2.5 %mul.16 = bf16[256,4096]{1,0:T(8,128)(2,1)S(1)} reshape(bf16[64,4,4096]{2,1,0:T(4,128)(2,1)} %broadcast_multiply_fusion) | data formatting | bytes 4194304 | tf_op jit(solution)/shard_map/mul | solution.py:40
  81.3 6.7 %fusion.2 = f32[256,1024]{1,0:T(8,128)} fusion(bf16[256,4096]{1,0:T(8,128)(2,1)S(1)} %mul.16, bf16[1,1024,4096]{2,1,0:T(8,128)(2,1)} %param.8, pred[1024]{0:T(1024)(128)(4,1)S(1)} %iota_compare_fusion), kind=kOutput, calls=%fused_computation.2 | convolution fusion | flops 2147745792 | bytes 11535360 | tf_op jit(solution)/shard_map/dot_general | solution.py:41
  88.0 0.0 reduce-scatter.2.cloned.1.call-update
  88.1 42.9 %reduce-scatter.2.cloned.1.call-done = f32[64,1024]{1,0:T(8,128)} async-done(((f32[256,1024]{1,0:T(8,128)}), f32[64,1024]{1,0:T(8,128)}) %reduce-scatter.2.cloned.1.call-update) | async-done | bytes 262160 | tf_op jit(solution)/shard_map/reduce_scatter | solution.py:46
  (2 shorter events, 0.0 us)
Async XLA Ops:
  6.5 1.7 %copy-start = (f32[1,64,64]{2,1,0:T(8,128)S(1)}, f32[1,64,64]{2,1,0:T(8,128)}, u32[]{:S(2)}) copy-start(f32[1,64,64]{2,1,0:T(8,128)} %param.10) | copy-start | bytes 49156
  13.4 12.7 %copy-start.1 = (s32[256,1]{0,1:T(1,128)S(1)}, s32[256,1]{0,1:T(1,128)}, u32[]{:S(2)}) copy-start(s32[256,1]{0,1:T(1,128)} %param.12) | copy-start | bytes 3076
  13.4 63.1 %all-to-all-start = ((bf16[64,4,4096]{2,1,0:T(4,128)(2,1)}), bf16[64,4,4096]{2,1,0:T(4,128)(2,1)S(1)}, u32[]{:S(2)}, u32[]{:S(2)}) async-start(bf16[64,4,4096]{2,1,0:T(4,128)(2,1)} %stack.2), calls=%async_computation | async-start | bytes 4194304 | tf_op jit(solution)/shard_map/all_to_all | solution.py:11
  26.1 104.9 %reduce-scatter.2.cloned.1.call-start = ((), (), s32[]{:S(2)}) async-start(), calls=%async_computation.2 | async-start | bytes 1310720 | tf_op jit(solution)/shard_map/reduce_scatter | solution.py:46
Sparse Core Ops, SparseCore 0:
  88.2 42.7 reduce-scatter.1
